TPU v7x, 32 devices: a whole 2x2x4 slice. The times are simulated.
32 devices in a mesh: node: 16 (over z, y, core), chip: 2 (over x).
Axes of the slice: x: 2, y: 2, z: 4, core: 2. Of those that a mesh axis runs over, the one named last changes fastest.
Arguments:
- tokens: bfloat16 [256, 3584], P(('node', 'chip')), may hold values from -6 to 6
- expert_ids: int32 [256, 8], P(('node', 'chip')), may hold values from 0 to 31, as said below
- gate_values: bfloat16 [256, 8], P(('node', 'chip')), may hold values from 0.099609375 to 1
- slot_ids: int32 [256, 8], P(('node', 'chip')), may hold values from 0 to 7, as said below
- up_weight: bfloat16 [32, 3584, 1024], P('node', None, 'chip'), may hold values from -0.09375 to 0.09375
- down_weight: bfloat16 [32, 1024, 3584], P('node', 'chip'), may hold values from -0.1875 to 0.1875
Outputs:
- mixed: bfloat16 [256, 3584], P(('node', 'chip'))
Inputs may be any that keep to these rules, and one draw needn't show every extreme that they name: `expert_ids`: each token's 8 entries name, in some order, all 2 experts of each of 4 distinct nodes. `slot_ids`: entries of one token that name experts of the same node hold the same slot; among the 16 tokens of one node (aligned blocks of the token dimension), the slots to one destination node are distinct, and some destination node receives all 8 slots from each source node.
All inputs are finite; a program needn't handle non-finite values.
Results may differ from a plain program's by a relative error of at most 0.0058.
Values may be sent and summed in bfloat16 or wider, within the bound.
A program may use at most 64 MiB of HBM per device.

v0:
```python
import jax
import jax.numpy as jnp
from jax import lax
from jax.sharding import PartitionSpec as P


def pack_rows(targets, experts, node_tokens, node_gates, row_count, per_node):
    row_ids = jnp.arange(row_count, dtype=jnp.int32)
    matches = (targets[None, :, :] == row_ids[:, None, None]).astype(jnp.bfloat16)
    picked = jnp.minimum(jnp.sum(matches.astype(jnp.float32), axis=2), 1.0).astype(jnp.bfloat16)
    packed = jnp.dot(picked, node_tokens, preferred_element_type=jnp.float32).astype(jnp.bfloat16)
    choose = (experts[:, :, None] == jnp.arange(per_node, dtype=jnp.int32)[None, None, :]).astype(
        jnp.bfloat16
    )
    weighted = choose * node_gates[:, :, None]
    gate_rows = jnp.einsum(
        "rtk,tke->re", matches, weighted, preferred_element_type=jnp.float32
    ).astype(jnp.bfloat16)
    return (packed, gate_rows)


def expert_rows(row_block, gate_block, up_local, down_local):
    result = jnp.zeros((row_block.shape[0], down_local.shape[2]), jnp.float32)
    for expert in range(up_local.shape[0]):
        hidden = jax.nn.silu(
            jnp.dot(row_block, up_local[expert], preferred_element_type=jnp.float32)
        ).astype(jnp.bfloat16)
        product = jnp.dot(hidden, down_local[expert], preferred_element_type=jnp.float32)
        result = result + gate_block[:, expert : expert + 1].astype(jnp.float32) * product
    return result.astype(jnp.bfloat16)


def gather_sum(indices, table):
    valid = indices >= 0
    safe = jnp.where(valid, indices, 0).reshape(-1)
    picked = jnp.take(table, safe, axis=0).reshape(
        indices.shape[0], indices.shape[1], table.shape[1]
    )
    return jnp.sum(jnp.where(valid[:, :, None], picked, 0.0), axis=1)


def shards(tokens, expert_ids, gate_values, slot_ids, up_weight, down_weight):
    node_count = lax.axis_size("node")
    chip_count = lax.axis_size("chip")
    my_chip = lax.axis_index("chip")
    tok_dev = tokens.shape[0]
    model_dim = tokens.shape[1]
    per_node = up_weight.shape[0]
    capacity = 8 * chip_count * tok_dev // node_count
    block_cap = capacity // chip_count
    route_code = (expert_ids // per_node * capacity + slot_ids) * per_node + expert_ids % per_node
    node_tokens, node_gates = (
        lax.all_gather(tokens, "chip", axis=0, tiled=True),
        lax.all_gather(gate_values, "chip", axis=0, tiled=True),
    )
    node_codes = lax.all_gather(route_code, "chip", axis=0, tiled=True)
    node_expert = node_codes % per_node
    node_slot = node_codes // per_node % capacity
    node_dest = node_codes // per_node // capacity
    targets = node_dest * capacity + node_slot
    packed, gate_rows = pack_rows(
        targets, node_expert, node_tokens, node_gates, node_count * capacity, per_node
    )
    shaped = packed.reshape(node_count, chip_count, 1, block_cap, model_dim)
    gate_shaped = gate_rows.reshape(node_count, chip_count, 1, block_cap, per_node)
    arrived, arrived_gates = (
        lax.all_to_all(shaped, "node", split_axis=0, concat_axis=2, tiled=True),
        lax.all_to_all(gate_shaped, "node", split_axis=0, concat_axis=2, tiled=True),
    )
    row_block = arrived.reshape(-1, model_dim)
    gate_block = arrived_gates.reshape(-1, per_node)
    partial_value = expert_rows(row_block, gate_block, up_weight, down_weight)
    pieces = lax.all_to_all(
        partial_value.reshape(chip_count, node_count * block_cap, model_dim),
        "chip",
        split_axis=0,
        concat_axis=0,
        tiled=True,
    )
    slot_sums = jnp.sum(pieces.astype(jnp.float32), axis=0).reshape(
        node_count, block_cap, model_dim
    )
    held = lax.all_to_all(slot_sums, "node", split_axis=0, concat_axis=0, tiled=True).reshape(
        node_count * block_cap, model_dim
    )
    wanted = (node_slot // block_cap == my_chip) & (node_expert == 0)
    indices = jnp.where(wanted, node_dest * block_cap + node_slot % block_cap, -1)
    term = gather_sum(indices, held)
    summed = lax.psum_scatter(term, "chip", scatter_dimension=0, tiled=True)
    return summed.astype(jnp.bfloat16)


def solution(mesh):
    return jax.shard_map(
        shards,
        mesh=mesh,
        in_specs=(
            P(("node", "chip"), None),
            P(("node", "chip"), None),
            P(("node", "chip"), None),
            P(("node", "chip"), None),
            P("node", None, "chip"),
            P("node", "chip", None),
        ),
        out_specs=P(("node", "chip"), None),
        check_vma=False,
    )
```

profile of v0, /device:TPU:0, one launch (start us, length us, event | category | flops | bytes accessed | tf_op | source)
XLA Modules:
  0.0 136.6 jit_solution(9596992641009980675)
XLA Ops:
  6.5 0.7 fusion.38
  7.3 5.3 %all_gather.9 = s32[16,8]{1,0:T(8,128)S(1)} all-gather(s32[8,8]{1,0:T(8,128)S(1)} %fusion.38), channel_id=1, replica_groups=mesh['node'=16,'chip'=2] {'chip'}, dimensions={0}, use_global_device_ids=true | all-gather | bytes 768 | tf_op jit(solution)/shard_map/all_gather | solution.py:56
  12.5 4.6 %all_gather.10 = bf16[16,8]{1,0:T(8,128)(2,1)S(1)} all-gather(bf16[8,8]{1,0:T(8,128)(2,1)} %param.8), channel_id=1, replica_groups=mesh['node'=16,'chip'=2] {'chip'}, dimensions={0}, use_global_device_ids=true | all-gather | bytes 384 | tf_op jit(solution)/shard_map/all_gather | solution.py:54
  17.1 0.1 copy.18
  17.2 0.1 copy.17
  17.3 0.1 copy.16
  17.4 0.2 fusion.14
  17.6 0.1 reshape.70
  17.7 0.6 copy.19
  18.3 6.4 %all-to-all-start = ((bf16[16,2,1,4,2]{3,1,4,2,0:T(2,128)(2,1)}), bf16[16,2,1,4,2]{3,1,4,2,0:T(2,128)(2,1)S(1)}, u32[]{:S(2)}, u32[]{:S(2)}) async-start(bf16[16,2,1,4,2]{3,1,4,2,0:T(2,128)(2,1)} %copy.19), calls=%async_computation | async-start | bytes 32768 | tf_op jit(solution)/shard_map/all_to_all | solution.py:68
  24.7 0.1 convert_reduce_fusion.1
  24.8 5.1 %all_gather.11 = bf16[16,3584]{1,0:T(8,128)(2,1)S(1)} all-gather(bf16[8,3584]{1,0:T(8,128)(2,1)} %param.6), channel_id=1, replica_groups=mesh['node'=16,'chip'=2] {'chip'}, dimensions={0}, use_global_device_ids=true | all-gather | bytes 172032 | tf_op jit(solution)/shard_map/all_gather | solution.py:53
  29.9 0.4 convolution_convert_fusion
  30.4 1.1 reshape.72
  31.5 0.0 all-to-all-done
  31.5 6.0 %all-to-all-start.1 = ((bf16[16,2,1,4,3584]{4,3,1,2,0:T(4,128)(2,1)}), bf16[16,2,1,4,3584]{4,3,1,2,0:T(4,128)(2,1)S(1)}, u32[]{:S(2)}, u32[]{:S(2)}) async-start(bf16[16,2,1,4,3584]{4,3,1,2,0:T(4,128)(2,1)} %bitcast.4), calls=%async_computation.1 | async-start | bytes 1835008 | tf_op jit(solution)/shard_map/all_to_all | solution.py:67
  37.5 0.1 reshape.71
  37.6 20.6 %all-to-all-done.1 = bf16[16,2,1,4,3584]{4,3,1,2,0:T(4,128)(2,1)S(1)} async-done(((bf16[16,2,1,4,3584]{4,3,1,2,0:T(4,128)(2,1)}), bf16[16,2,1,4,3584]{4,3,1,2,0:T(4,128)(2,1)S(1)}, u32[]{:S(2)}, u32[]{:S(2)}) %all-to-all-start.1) | async-done | bytes 917536 | tf_op jit(solution)/shard_map/all_to_all | solution.py:67
  58.3 0.3 copy.22
  58.6 0.2 reshape.73
  58.8 5.7 %convolution_multiply_fusion.1 = f32[128,3584]{1,0:T(8,128)} fusion(bf16[2,512,3584]{2,1,0:T(8,128)(2,1)} %param.11, f32[128]{0:T(128)S(1)} %get-tuple-element.10, bf16[128,3584]{1,0:T(8,128)(2,1)S(1)} %reshape.73, bf16[2,3584,512]{2,1,0:T(8,128)(2,1)} %param.10), kind=kOutput, calls=%fused_computation.3 | convolution fusion | flops 940310528 | bytes 10093056 | tf_op jit(solution)/shard_map/dot_general | solution.py:28
  64.5 4.9 %fusion.1 = bf16[128,3584]{1,0:T(8,128)(2,1)S(1)} fusion(f32[128,3584]{1,0:T(8,128)} %convolution_multiply_fusion.1, bf16[2,512,3584]{2,1,0:T(8,128)(2,1)} %param.11, f32[128]{0:T(128)S(1)} %get-tuple-element.9, bf16[128,3584]{1,0:T(8,128)(2,1)S(1)} %reshape.73, bf16[2,3584,512]{2,1,0:T(8,128)(2,1)} %param.10), kind=kOutput, calls=%fused_computation.4 | convolution fusion | flops 941228032 | bytes 11010560 | tf_op jit(solution)/shard_map/dot_general | solution.py:28
  69.5 15.6 %all_to_all.40 = bf16[2,64,3584]{2,1,0:T(8,128)(2,1)S(1)} all-to-all(bf16[2,64,3584]{2,1,0:T(8,128)(2,1)S(1)} %bitcast.58), channel_id=1, replica_groups=mesh['node'=16,'chip'=2] {'chip'}, dimensions={0} | all-to-all | bytes 1835008 | tf_op jit(solution)/shard_map/all_to_all | solution.py:73
  85.1 0.1 convert_reduce_fusion
  85.2 1.2 reshape.75
  86.4 5.9 %all-to-all-start.3 = ((f32[16,4,3584]{2,1,0:T(4,128)}), f32[16,4,3584]{2,1,0:T(4,128)S(1)}, u32[]{:S(2)}, u32[]{:S(2)}) async-start(f32[16,4,3584]{2,1,0:T(4,128)} %reshape.75), calls=%async_computation.3 | async-start | bytes 1835008 | tf_op jit(solution)/shard_map/all_to_all | solution.py:83
  92.4 0.0 reduce-scatter.2.cloned.1.call-start
  92.5 0.1 reshape.77
  92.6 20.5 %all-to-all-done.3 = f32[16,4,3584]{2,1,0:T(4,128)S(1)} async-done(((f32[16,4,3584]{2,1,0:T(4,128)}), f32[16,4,3584]{2,1,0:T(4,128)S(1)}, u32[]{:S(2)}, u32[]{:S(2)}) %all-to-all-start.3) | async-done | bytes 917536 | tf_op jit(solution)/shard_map/all_to_all | solution.py:83
  113.1 0.3 reshape.76
  113.5 1.3 gather_fusion
  114.7 1.4 %fusion.13 = f32[16,3584]{1,0:T(8,128)} fusion(f32[128,3584]{1,0:T(8,128)S(1)} %gather_fusion, pred[16,8]{1,0:T(8,128)(4,1)S(1)} %compare_and_fusion, pred[16,8]{1,0:T(8,128)(4,1)S(1)} %get-tuple-element.5), kind=kLoop, calls=%fused_computation.18 | loop fusion | flops 1318912 | bytes 2064640 | tf_op jit(solution)/shard_map/reduce_sum | solution.py:39
  116.2 0.0 reduce-scatter.2.cloned.1.call-update
  116.2 12.0 %reduce-scatter.2.cloned.1.call-done = f32[8,3584]{1,0:T(8,128)} async-done(((f32[16,3584]{1,0:T(8,128)}), f32[8,3584]{1,0:T(8,128)}) %reduce-scatter.2.cloned.1.call-update) | async-done | bytes 114704 | tf_op jit(solution)/shard_map/reduce_scatter | solution.py:89
  128.2 1.5 %convert_element_type.42 = bf16[8,3584]{1,0:T(8,128)(2,1)} convert(f32[8,3584]{1,0:T(8,128)} %reduce-scatter.2.cloned.1.call-done) | non-fusion elementwise | flops 28672 | bytes 172032 | tf_op jit(solution)/shard_map/convert_element_type | solution.py:90
  (8 shorter events, 0.1 us)
Async XLA Ops:
  18.3 13.2 %all-to-all-start = ((bf16[16,2,1,4,2]{3,1,4,2,0:T(2,128)(2,1)}), bf16[16,2,1,4,2]{3,1,4,2,0:T(2,128)(2,1)S(1)}, u32[]{:S(2)}, u32[]{:S(2)}) async-start(bf16[16,2,1,4,2]{3,1,4,2,0:T(2,128)(2,1)} %copy.19), calls=%async_computation | async-start | bytes 32768 | tf_op jit(solution)/shard_map/all_to_all | solution.py:68
  31.5 26.8 %all-to-all-start.1 = ((bf16[16,2,1,4,3584]{4,3,1,2,0:T(4,128)(2,1)}), bf16[16,2,1,4,3584]{4,3,1,2,0:T(4,128)(2,1)S(1)}, u32[]{:S(2)}, u32[]{:S(2)}) async-start(bf16[16,2,1,4,3584]{4,3,1,2,0:T(4,128)(2,1)} %bitcast.4), calls=%async_computation.1 | async-start | bytes 1835008 | tf_op jit(solution)/shard_map/all_to_all | solution.py:67
  86.4 26.7 %all-to-all-start.3 = ((f32[16,4,3584]{2,1,0:T(4,128)}), f32[16,4,3584]{2,1,0:T(4,128)S(1)}, u32[]{:S(2)}, u32[]{:S(2)}) async-start(f32[16,4,3584]{2,1,0:T(4,128)} %reshape.75), calls=%async_computation.3 | async-start | bytes 1835008 | tf_op jit(solution)/shard_map/all_to_all | solution.py:83
  92.4 35.9 %reduce-scatter.2.cloned.1.call-start = ((), (), s32[]{:S(2)}) async-start(), calls=%async_computation.5 | async-start | bytes 344064 | tf_op jit(solution)/shard_map/reduce_scatter | solution.py:89
Sparse Core Ops, SparseCore 0:
  116.3 11.8 reduce-scatter.1
where the time goes:
time: 137 us
  waiting for transfers between devices  53.3 us (39%)
  blocking collectives  30.6 us (22%)
  starting transfers between devices  18.4 us (13%)
  between operations  13.5 us (10%)
  matrix products  11.3 us (8%)
  local copies, waits for them, and re-layouts  5.6 us (4%)
  other arithmetic  3.99 us (3%)
    all_to_all x1, waiting for transfers between devices, shards(): lax.all_to_all(shaped, 'node', split_axis=0, concat_axis=2, tiled=True)  20.6 us
    all_to_all x1, waiting for transfers between devices, shards(): lax.all_to_all(slot_sums, 'node', split_axis=0, concat_axis=0, tiled=True)  20.5 us
    all_to_all x1, blocking collectives, shards(): lax.all_to_all(partial_value.reshape(chip_count, node_count * block_cap,...  15.6 us
    reduce_scatter x1, waiting for transfers between devices, shards(): summed = lax.psum_scatter(term, 'chip', scatter_dimension=0, tiled=True)  12 us
    dot_general x2, matrix products, expert_rows(): jnp.dot(hidden, down_local[expert], preferred_element_type=jnp.float32)  10.7 us
    all_to_all x1, starting transfers between devices, shards(): lax.all_to_all(gate_shaped, 'node', split_axis=0, concat_axis=2, tiled=True)  6.42 us
    all_to_all x1, starting transfers between devices, shards(): lax.all_to_all(shaped, 'node', split_axis=0, concat_axis=2, tiled=True)  5.97 us
    all_to_all x1, starting transfers between devices, shards(): lax.all_to_all(slot_sums, 'node', split_axis=0, concat_axis=0, tiled=True)  5.95 us
  transfers between devices with their start and end apart: 4, of which 3 were waited for; matrix products, arithmetic and copies ran while one was open for 1% of the time, Pallas kernels for 0%

commit v1 on v0

--- a/solution.py
+++ b/solution.py
@@ -1,6 +1,10 @@
+import functools
+
 import jax
 import jax.numpy as jnp
 from jax import lax
+from jax.experimental import pallas as pl
+from jax.experimental.pallas import tpu as pltpu
 from jax.sharding import PartitionSpec as P
 
 
@@ -90,9 +94,324 @@
     return summed.astype(jnp.bfloat16)
 
 
+LANES = 128
+PIECES = 4
+MESH = pl.DeviceIdType.MESH
+
+
+def fused_kernel(
+    nz, tokens_ref, ids_ref, gates_ref, up_hbm, down_hbm, out_ref,
+    up_v, down_v, gath, rows_v, hid_v, total,
+    core_out, core_in, one_out, one_in, two_out, two_in, z_out, z_in,
+    local_sem, up_sem, down_sem,
+    gz_send, gz_recv, g1_send, g1_recv, g2_send, g2_recv, gc_send, gc_recv,
+    r_send, r_recv,
+):
+    f32, bf16 = jnp.float32, jnp.bfloat16
+    node, x = lax.axis_index("node"), lax.axis_index("chip")
+    c = lax.rem(node, 2)
+    y = lax.rem(lax.div(node, 2), 2)
+    z = lax.div(node, 4)
+    model = tokens_ref.shape[1]
+    per_node = up_v.shape[0]
+    half = model // 2
+    piece = model // PIECES
+    blocks = 8 * nz
+    per_core = 4 * nz
+
+    def dev(zz, yy, cc, xx):
+        return ((zz * 2 + yy) * 2 + cc, xx)
+
+    def block(cc, xx, yy, zz):
+        return ((cc * 2 + xx) * 2 + yy) * nz + zz
+
+    def z_peer(j):
+        return dev(lax.rem(z + j, nz), y, c, x)
+
+    x_peer, y_peer, c_peer = dev(z, y, c, 1 - x), dev(z, 1 - y, c, x), dev(z, y, 1 - c, x)
+
+    own = block(c, x, y, z)
+    stage = pltpu.make_async_copy(tokens_ref, gath.at[own, :, pl.ds(0, model)], local_sem)
+    stage.start()
+    up_copies = []
+    down_copies = []
+    for e in range(per_node):
+        up_copies.append(pltpu.make_async_copy(up_hbm.at[e], up_v.at[e], up_sem.at[e]))
+        down_copies.append(pltpu.make_async_copy(down_hbm.at[e], down_v.at[e], down_sem.at[e]))
+
+    lanes = lax.broadcasted_iota(jnp.int32, (tokens_ref.shape[0], LANES), 1)
+    table = jnp.zeros((tokens_ref.shape[0], LANES), f32)
+    ids = ids_ref[...]
+    gates = gates_ref[...].astype(f32)
+    for k in range(ids.shape[1]):
+        table = table + jnp.where(ids[:, k : k + 1] == lanes, gates[:, k : k + 1], 0.0)
+    gath[own, :, pl.ds(model, LANES)] = table.astype(bf16)
+
+    barrier = pltpu.get_barrier_semaphore()
+    peers = [z_peer(j) for j in range(1, nz)] + [y_peer, x_peer, c_peer]
+    for peer in peers:
+        pl.semaphore_signal(barrier, inc=1, device_id=peer, device_id_type=MESH)
+    stage.wait()
+    pl.semaphore_wait(barrier, len(peers))
+
+    spans = [pl.ds(0, half), pl.ds(half, half + LANES)]
+    sends = []
+
+    def send(src, dst, ssem, rsem, peer):
+        copy = pltpu.make_async_remote_copy(
+            src_ref=src, dst_ref=dst, send_sem=ssem, recv_sem=rsem,
+            device_id=peer, device_id_type=MESH,
+        )
+        copy.start()
+        sends.append(copy)
+        return copy
+
+    def gsend(h, b, ssem, rsem, peer):
+        ref = gath.at[b, :, spans[h]]
+        return send(ref, ref, ssem, rsem, peer)
+
+    firsts = [y_peer, x_peer]
+    seconds = [x_peer, y_peer]
+
+    def mine(h, k):
+        return block(c, x, y, lax.rem(z + nz - k, nz))
+
+    def other(h, k):
+        zz = lax.rem(z + nz - k, nz)
+        return block(c, x, 1 - y, zz) if h == 0 else block(c, 1 - x, y, zz)
+
+    zc = {}
+    first = {}
+    second = {}
+    for h in range(2):
+        for j in range(1, nz):
+            zc[h, j] = gsend(h, own, gz_send.at[h, j - 1], gz_recv.at[h, j - 1], z_peer(j))
+
+    def forward_mine(h, k):
+        if k:
+            zc[h, k].wait_recv()
+        first[h, k] = gsend(h, mine(h, k), g1_send.at[h, k], g1_recv.at[h, k], firsts[h])
+        second[h, k] = gsend(h, mine(h, k), g2_send.at[h, k], g2_recv.at[h, k], seconds[h])
+
+    def forward_other(h, k):
+        first[h, k].wait_recv()
+        second[h, nz + k] = gsend(
+            h, other(h, k), g2_send.at[h, nz + k], g2_recv.at[h, nz + k], seconds[h]
+        )
+
+    corec = {}
+
+    def share(h, g, xx, yy):
+        ref = gath.at[pl.ds(block(c, xx, yy, 0), nz), :, spans[h]]
+        corec[h, g] = send(ref, ref, gc_send.at[h, g], gc_recv.at[h, g], c_peer)
+
+    forward_mine(0, 0)
+    forward_mine(1, 0)
+    for copy in up_copies + down_copies:
+        copy.start()
+    for k in range(1, nz):
+        for h in range(2):
+            forward_mine(h, k)
+        for h in range(2):
+            forward_other(h, k - 1)
+    for h in range(2):
+        share(h, 0, x, y)
+    for h in range(2):
+        forward_other(h, nz - 1)
+    share(0, 1, x, 1 - y)
+    share(1, 1, 1 - x, y)
+    for g in range(2):
+        for h in range(2):
+            for k in range(nz):
+                second[h, g * nz + k].wait_recv()
+        if g == 0:
+            share(0, 2, 1 - x, y)
+            share(1, 2, x, 1 - y)
+        else:
+            share(0, 3, 1 - x, 1 - y)
+            share(1, 3, 1 - x, 1 - y)
+    for copy in corec.values():
+        copy.wait_recv()
+    for copy in sends:
+        copy.wait_send()
+
+    def pack(i, carry):
+        pair = gath[pl.ds(2 * i, 2), :, pl.ds(0, model)].astype(f32)
+        flat = pair.reshape(2 * pair.shape[1], model).astype(bf16)
+        rows_v[pl.ds(pl.multiple_of(16 * i, 16), 16), :] = flat
+        return carry
+
+    lax.fori_loop(0, blocks // 2, pack, 0)
+    table = gath[:, :, pl.ds(model, LANES)].astype(f32).reshape(rows_v.shape[0], LANES)
+    lane = lax.broadcasted_iota(jnp.int32, table.shape, 1)
+    weight = [
+        jnp.sum(jnp.where(lane == node * per_node + e, table, 0.0), axis=1, keepdims=True)
+        for e in range(per_node)
+    ]
+
+    for copy in up_copies:
+        copy.wait()
+
+    def up_step(e, carry):
+        value = jnp.dot(rows_v[...], up_v[e], preferred_element_type=f32)
+        hid_v[e] = (value / (1.0 + jnp.exp(-value))).astype(bf16)
+        return carry
+
+    lax.fori_loop(0, per_node, up_step, 0)
+    for copy in down_copies:
+        copy.wait()
+
+    rsends = []
+    corer, oner, twor, zr = {}, {}, {}, {}
+
+    def rsend(src, dst, q, s, peer):
+        copy = pltpu.make_async_remote_copy(
+            src_ref=src, dst_ref=dst, send_sem=r_send.at[q, s], recv_sem=r_recv.at[q, s],
+            device_id=peer, device_id_type=MESH,
+        )
+        copy.start()
+        rsends.append(copy)
+        return copy
+
+    def produce(q):
+        cols = pl.ds(q * piece, piece)
+        value = weight[0] * jnp.dot(hid_v[0], down_v[0, :, cols], preferred_element_type=f32)
+        for e in range(1, per_node):
+            value = value + weight[e] * jnp.dot(
+                hid_v[e], down_v[e, :, cols], preferred_element_type=f32
+            )
+        total[q] = value.reshape(blocks, rows_v.shape[0] // blocks, piece)
+        core_out[q] = total[q, pl.ds((1 - c) * per_core, per_core)].astype(bf16)
+        corer[q] = rsend(core_out.at[q], core_in.at[q], q, 0, c_peer)
+
+    def after_core(q):
+        corer[q].wait_recv()
+        base = c * per_core
+        if q % 2 == 0:
+            far = pl.ds(base + (1 - x) * 2 * nz, 2 * nz)
+            near = pl.ds(base + x * 2 * nz, 2 * nz)
+            one_out[q] = (
+                total[q, far] + core_in[q, pl.ds((1 - x) * 2 * nz, 2 * nz)].astype(f32)
+            ).astype(bf16)
+            oner[q] = rsend(one_out.at[q], one_in.at[q], q, 1, x_peer)
+            total[q, near] += core_in[q, pl.ds(x * 2 * nz, 2 * nz)].astype(f32)
+        else:
+            for xx in range(2):
+                off = xx * 2 * nz + (1 - y) * nz
+                one_out[q, xx * nz : (xx + 1) * nz] = (
+                    total[q, pl.ds(base + off, nz)] + core_in[q, pl.ds(off, nz)].astype(f32)
+                ).astype(bf16)
+            oner[q] = rsend(one_out.at[q], one_in.at[q], q, 1, y_peer)
+            for xx in range(2):
+                off = xx * 2 * nz + y * nz
+                total[q, pl.ds(base + off, nz)] += core_in[q, pl.ds(off, nz)].astype(f32)
+
+    def after_one(q):
+        oner[q].wait_recv()
+        near = pl.ds(block(c, x, y, 0), nz)
+        if q % 2 == 0:
+            far, slot_far, slot_near, peer = block(c, x, 1 - y, 0), 1 - y, y, y_peer
+        else:
+            far, slot_far, slot_near, peer = block(c, 1 - x, y, 0), 1 - x, x, x_peer
+        two_out[q] = (
+            total[q, pl.ds(far, nz)] + one_in[q, pl.ds(slot_far * nz, nz)].astype(f32)
+        ).astype(bf16)
+        twor[q] = rsend(two_out.at[q], two_in.at[q], q, 2, peer)
+        total[q, near] += one_in[q, pl.ds(slot_near * nz, nz)].astype(f32)
+
+    def after_two(q):
+        twor[q].wait_recv()
+        base = block(c, x, y, 0)
+        for j in range(1, nz):
+            zz = lax.rem(z + j, nz)
+            z_out[q, j - 1] = (total[q, base + zz] + two_in[q, zz].astype(f32)).astype(bf16)
+            zr[q, j] = rsend(
+                z_out.at[q, j - 1], z_in.at[q, j - 1], q, 2 + j, z_peer(j)
+            )
+        total[q, base + z] += two_in[q, z].astype(f32)
+
+    def finish(q):
+        value = total[q, own]
+        for j in range(1, nz):
+            zr[q, j].wait_recv()
+            value = value + z_in[q, j - 1].astype(f32)
+        out_ref[:, pl.ds(q * piece, piece)] = value.astype(out_ref.dtype)
+
+    steps = [produce, after_core, after_one, after_two, finish]
+    for t in range(PIECES + len(steps) - 1):
+        for s, step in enumerate(steps):
+            if 0 <= t - s < PIECES:
+                step(t - s)
+    for copy in rsends:
+        copy.wait_send()
+
+
+def fused(nz, tokens, expert_ids, gate_values, slot_ids, up_weight, down_weight):
+    tok, model = tokens.shape
+    per_node, _, width = up_weight.shape
+    blocks = 8 * nz
+    piece = model // PIECES
+    bf16, f32 = jnp.bfloat16, jnp.float32
+    vmem = pl.BlockSpec(memory_space=pltpu.VMEM)
+    anyspace = pl.BlockSpec(memory_space=pl.ANY)
+    dma = pltpu.SemaphoreType.DMA
+
+    def pieces(n):
+        return pltpu.VMEM((PIECES, n, tok, piece), bf16)
+
+    return pl.pallas_call(
+        functools.partial(fused_kernel, nz),
+        out_shape=jax.ShapeDtypeStruct((tok, model), bf16),
+        in_specs=[anyspace, vmem, vmem, anyspace, anyspace],
+        out_specs=vmem,
+        scratch_shapes=[
+            pltpu.VMEM(up_weight.shape, bf16),
+            pltpu.VMEM(down_weight.shape, bf16),
+            pltpu.VMEM((blocks, tok, model + LANES), bf16),
+            pltpu.VMEM((blocks * tok, model), bf16),
+            pltpu.VMEM((per_node, blocks * tok, width), bf16),
+            pltpu.VMEM((PIECES, blocks, tok, piece), f32),
+            pieces(4 * nz), pieces(4 * nz),
+            pieces(2 * nz), pieces(2 * nz),
+            pieces(nz), pieces(nz),
+            pieces(nz - 1), pieces(nz - 1),
+            dma, dma((per_node,)), dma((per_node,)),
+            dma((2, nz - 1)), dma((2, nz - 1)),
+            dma((2, nz)), dma((2, nz)),
+            dma((2, 2 * nz)), dma((2, 2 * nz)),
+            dma((2, 4)), dma((2, 4)),
+            dma((PIECES, 2 + nz)), dma((PIECES, 2 + nz)),
+        ],
+        compiler_params=pltpu.CompilerParams(
+            collective_id=0, has_side_effects=True, vmem_limit_bytes=60 * 1024 * 1024
+        ),
+    )(tokens, expert_ids, gate_values, up_weight, down_weight)
+
+
+def body_for(mesh):
+    nodes, chips = mesh.shape["node"], mesh.shape["chip"]
+    nz = nodes // 4
+
+    def body(tokens, expert_ids, gate_values, slot_ids, up_weight, down_weight):
+        tok, model = tokens.shape
+        experts = nodes * up_weight.shape[0]
+        if (
+            chips == 2
+            and nodes == 4 * nz
+            and 2 <= nz <= 4
+            and tok == 8
+            and model % (PIECES * LANES) == 0
+            and experts <= LANES
+        ):
+            return fused(nz, tokens, expert_ids, gate_values, slot_ids, up_weight, down_weight)
+        return shards(tokens, expert_ids, gate_values, slot_ids, up_weight, down_weight)
+
+    return body
+
+
 def solution(mesh):
     return jax.shard_map(
-        shards,
+        body_for(mesh),
         mesh=mesh,
         in_specs=(
             P(("node", "chip"), None),

time: 137 us -> 49.3 us (0.36)
  waiting for transfers between devices: 53.3 us -> 0 us
  Pallas kernels: 0 us -> 47.6 us
  blocking collectives: 30.6 us -> 0 us
  starting transfers between devices: 18.4 us -> 0 us
  between operations: 13.5 us -> 0.01 us
  matrix products: 11.3 us -> 0 us
  local copies, waits for them, and re-layouts: 5.6 us -> 1.45 us
  other arithmetic: 3.99 us -> 0 us
    pallas_call x0 -> x1, Pallas kernels: none -> 47.6 us  [fused(): pl.pallas_call(functools.partial(fused_kernel, nz), out_shape=jax.ShapeDt...]
    all_to_all x3 -> x0, waiting for transfers between devices: 41.2 us -> none  [the longest x1 20.6 us: shards(): lax.all_to_all(shaped, 'node', split_axis=0, concat_axis=2, tiled=True)]
    all_to_all x3 -> x0, starting transfers between devices: 18.3 us -> none  [the longest x1 6.42 us: shards(): lax.all_to_all(gate_shaped, 'node', split_axis=0, concat_axis=2, tiled=True)]
    all_to_all x1 -> x0, blocking collectives: 15.6 us -> none  [shards(): lax.all_to_all(partial_value.reshape(chip_count, node_count * block_cap,...]
    all_gather x3 -> x0, blocking collectives: 15 us -> none  [the longest x1 5.28 us: shards(): node_codes = lax.all_gather(route_code, 'chip', axis=0, tiled=True)]
    reduce_scatter x1 -> x0, waiting for transfers between devices: 12 us -> none  [shards(): summed = lax.psum_scatter(term, 'chip', scatter_dimension=0, tiled=True)]
    dot_general x4 -> x0, matrix products: 11.3 us -> none  [the longest x2 10.7 us: expert_rows(): jnp.dot(hidden, down_local[expert], preferred_element_type=jnp.float32)]
    reshape x8 -> x0, local copies, waits for them, and re-layouts: 3.81 us -> none  [the longest x1 1.2 us: shards(): jnp.sum(pieces.astype(jnp.float32), axis=0)]
  transfers between devices with their start and end apart: 4 -> 0, of which waited for: 3 -> 0; matrix products, arithmetic and copies ran while one was open for 1% -> 0% of each run, Pallas kernels for 0% -> 0%
where the time goes in v1:
time: 49.3 us; the launch traced here: 49 us
  Pallas kernels  47.6 us (97%)
  local copies, waits for them, and re-layouts  1.45 us (3%)
    pallas_call x1, Pallas kernels, fused(): pl.pallas_call(functools.partial(fused_kernel, nz), out_shape=jax.ShapeDt...  47.6 us
    unnamed x1, local copies, waits for them, and re-layouts  1.45 us

profile of v1, /device:TPU:0, one launch (start us, length us, event | category | flops | bytes accessed | tf_op | source)
XLA Modules:
  0.0 49.0 jit_solution(15989303858416237231)
XLA Ops:
  0.0 47.6 %shard_map.55 = bf16[8,3584]{1,0:T(8,128)(2,1)} custom-call(bf16[8,3584]{1,0:T(8,128)(2,1)} %tokens_ref.1, s32[8,8]{1,0:T(8,128)} %ids_ref.1, bf16[8,8]{1,0:T(8,128)(2,1)} %gates_ref.1, bf16[2,3584,512]{2,1,0:T(8,128)(2,1)} %up_hbm.1, bf16[2,512,3584]{2,1,0:T(8,128)(2,1)} %down_hbm.1), custom_call_target="tpu_custom_call" | custom-call | tf_op jit(solution)/shard_map/pallas_call | solution.py:362
  47.6 1.4 %copy.7 = bf16[8,3584]{1,0:T(8,128)(2,1)} copy(bf16[8,3584]{1,0:T(8,128)(2,1)} %shard_map.55) | data formatting | bytes 114688

commit v2 on v1

--- a/solution.py
+++ b/solution.py
@@ -102,9 +102,9 @@
 def fused_kernel(
     nz, tokens_ref, ids_ref, gates_ref, up_hbm, down_hbm, out_ref,
     up_v, down_v, gath, rows_v, hid_v, total,
-    core_out, core_in, one_out, one_in, two_out, two_in, z_out, z_in,
+    core_out, core_in, plane_out, plane_in, z_out, z_in,
     local_sem, up_sem, down_sem,
-    gz_send, gz_recv, g1_send, g1_recv, g2_send, g2_recv, gc_send, gc_recv,
+    gz_send, gz_recv, ge_send, ge_recv, gp_send, gp_recv, gf_send, gf_recv, gc_send, gc_recv,
     r_send, r_recv,
 ):
     f32, bf16 = jnp.float32, jnp.bfloat16
@@ -114,7 +114,6 @@
     z = lax.div(node, 4)
     model = tokens_ref.shape[1]
     per_node = up_v.shape[0]
-    half = model // 2
     piece = model // PIECES
     blocks = 8 * nz
     per_core = 4 * nz
@@ -128,7 +127,9 @@
     def z_peer(j):
         return dev(lax.rem(z + j, nz), y, c, x)
 
-    x_peer, y_peer, c_peer = dev(z, y, c, 1 - x), dev(z, 1 - y, c, x), dev(z, y, 1 - c, x)
+    c_peer = dev(z, y, 1 - c, x)
+    plane_at = [(1 - x, 1 - y), (1 - x, y), (x, 1 - y)]
+    plane_peers = [dev(z, yy, c, xx) for xx, yy in plane_at]
 
     own = block(c, x, y, z)
     stage = pltpu.make_async_copy(tokens_ref, gath.at[own, :, pl.ds(0, model)], local_sem)
@@ -148,13 +149,12 @@
     gath[own, :, pl.ds(model, LANES)] = table.astype(bf16)
 
     barrier = pltpu.get_barrier_semaphore()
-    peers = [z_peer(j) for j in range(1, nz)] + [y_peer, x_peer, c_peer]
+    peers = [z_peer(j) for j in range(1, nz)] + plane_peers + [c_peer]
     for peer in peers:
         pl.semaphore_signal(barrier, inc=1, device_id=peer, device_id_type=MESH)
     stage.wait()
     pl.semaphore_wait(barrier, len(peers))
 
-    spans = [pl.ds(0, half), pl.ds(half, half + LANES)]
     sends = []
 
     def send(src, dst, ssem, rsem, peer):
@@ -166,71 +166,55 @@
         sends.append(copy)
         return copy
 
-    def gsend(h, b, ssem, rsem, peer):
-        ref = gath.at[b, :, spans[h]]
+    early = pl.ds(0, piece)
+    late = pl.ds(piece, model + LANES - piece)
+
+    def gsend(ref, ssem, rsem, peer):
         return send(ref, ref, ssem, rsem, peer)
 
-    firsts = [y_peer, x_peer]
-    seconds = [x_peer, y_peer]
-
-    def mine(h, k):
-        return block(c, x, y, lax.rem(z + nz - k, nz))
-
-    def other(h, k):
-        zz = lax.rem(z + nz - k, nz)
-        return block(c, x, 1 - y, zz) if h == 0 else block(c, 1 - x, y, zz)
-
-    zc = {}
-    first = {}
-    second = {}
-    for h in range(2):
-        for j in range(1, nz):
-            zc[h, j] = gsend(h, own, gz_send.at[h, j - 1], gz_recv.at[h, j - 1], z_peer(j))
-
-    def forward_mine(h, k):
+    def behind(k):
+        return lax.rem(z + nz - k, nz)
+
+    zc, plane, ec, ez, shared = {}, {}, {}, {}, []
+    for j in range(1, nz):
+        zc[j] = gsend(gath.at[own, :, late], gz_send.at[j - 1], gz_recv.at[j - 1], z_peer(j))
+    for p in range(3):
+        ec[p] = gsend(gath.at[own, :, early], ge_send.at[p], ge_recv.at[p], plane_peers[p])
+
+    def forward_late(k):
         if k:
-            zc[h, k].wait_recv()
-        first[h, k] = gsend(h, mine(h, k), g1_send.at[h, k], g1_recv.at[h, k], firsts[h])
-        second[h, k] = gsend(h, mine(h, k), g2_send.at[h, k], g2_recv.at[h, k], seconds[h])
-
-    def forward_other(h, k):
-        first[h, k].wait_recv()
-        second[h, nz + k] = gsend(
-            h, other(h, k), g2_send.at[h, nz + k], g2_recv.at[h, nz + k], seconds[h]
-        )
-
-    corec = {}
-
-    def share(h, g, xx, yy):
-        ref = gath.at[pl.ds(block(c, xx, yy, 0), nz), :, spans[h]]
-        corec[h, g] = send(ref, ref, gc_send.at[h, g], gc_recv.at[h, g], c_peer)
-
-    forward_mine(0, 0)
-    forward_mine(1, 0)
+            zc[k].wait_recv()
+        ref = gath.at[block(c, x, y, behind(k)), :, late]
+        for p in range(3):
+            plane[p, k] = gsend(ref, gp_send.at[p, k], gp_recv.at[p, k], plane_peers[p])
+
+    def forward_early(g):
+        if g:
+            ec[g - 1].wait_recv()
+        xx, yy = plane_at[g - 1] if g else (x, y)
+        ref = gath.at[block(c, xx, yy, z), :, early]
+        for j in range(1, nz):
+            ez[g, j] = gsend(ref, gf_send.at[g, j - 1], gf_recv.at[g, j - 1], z_peer(j))
+
+    forward_late(0)
+    forward_early(0)
     for copy in up_copies + down_copies:
         copy.start()
     for k in range(1, nz):
-        for h in range(2):
-            forward_mine(h, k)
-        for h in range(2):
-            forward_other(h, k - 1)
-    for h in range(2):
-        share(h, 0, x, y)
-    for h in range(2):
-        forward_other(h, nz - 1)
-    share(0, 1, x, 1 - y)
-    share(1, 1, 1 - x, y)
-    for g in range(2):
-        for h in range(2):
+        forward_late(k)
+        if k == 1:
+            for g in range(1, 4):
+                forward_early(g)
+    for g in range(4):
+        xx, yy = plane_at[g - 1] if g else (x, y)
+        for j in range(1, nz):
+            ez[g, j].wait_recv()
+        if g:
             for k in range(nz):
-                second[h, g * nz + k].wait_recv()
-        if g == 0:
-            share(0, 2, 1 - x, y)
-            share(1, 2, x, 1 - y)
-        else:
-            share(0, 3, 1 - x, 1 - y)
-            share(1, 3, 1 - x, 1 - y)
-    for copy in corec.values():
+                plane[g - 1, k].wait_recv()
+        ref = gath.at[pl.ds(block(c, xx, yy, 0), nz)]
+        shared.append(gsend(ref, gc_send.at[g], gc_recv.at[g], c_peer))
+    for copy in shared:
         copy.wait_recv()
     for copy in sends:
         copy.wait_send()
@@ -262,7 +246,7 @@
         copy.wait()
 
     rsends = []
-    corer, oner, twor, zr = {}, {}, {}, {}
+    corer, planer, zr = {}, {}, {}
 
     def rsend(src, dst, q, s, peer):
         copy = pltpu.make_async_remote_copy(
@@ -286,49 +270,30 @@
 
     def after_core(q):
         corer[q].wait_recv()
-        base = c * per_core
-        if q % 2 == 0:
-            far = pl.ds(base + (1 - x) * 2 * nz, 2 * nz)
-            near = pl.ds(base + x * 2 * nz, 2 * nz)
-            one_out[q] = (
-                total[q, far] + core_in[q, pl.ds((1 - x) * 2 * nz, 2 * nz)].astype(f32)
+        for p, (xx, yy) in enumerate(plane_at):
+            slots = pl.ds(p * nz, nz)
+            plane_out[q, slots] = (
+                total[q, pl.ds(block(c, xx, yy, 0), nz)]
+                + core_in[q, pl.ds(block(0, xx, yy, 0), nz)].astype(f32)
             ).astype(bf16)
-            oner[q] = rsend(one_out.at[q], one_in.at[q], q, 1, x_peer)
-            total[q, near] += core_in[q, pl.ds(x * 2 * nz, 2 * nz)].astype(f32)
-        else:
-            for xx in range(2):
-                off = xx * 2 * nz + (1 - y) * nz
-                one_out[q, xx * nz : (xx + 1) * nz] = (
-                    total[q, pl.ds(base + off, nz)] + core_in[q, pl.ds(off, nz)].astype(f32)
-                ).astype(bf16)
-            oner[q] = rsend(one_out.at[q], one_in.at[q], q, 1, y_peer)
-            for xx in range(2):
-                off = xx * 2 * nz + y * nz
-                total[q, pl.ds(base + off, nz)] += core_in[q, pl.ds(off, nz)].astype(f32)
-
-    def after_one(q):
-        oner[q].wait_recv()
+            planer[q, p] = rsend(
+                plane_out.at[q, slots], plane_in.at[q, slots], q, 1 + p, plane_peers[p]
+            )
         near = pl.ds(block(c, x, y, 0), nz)
-        if q % 2 == 0:
-            far, slot_far, slot_near, peer = block(c, x, 1 - y, 0), 1 - y, y, y_peer
-        else:
-            far, slot_far, slot_near, peer = block(c, 1 - x, y, 0), 1 - x, x, x_peer
-        two_out[q] = (
-            total[q, pl.ds(far, nz)] + one_in[q, pl.ds(slot_far * nz, nz)].astype(f32)
-        ).astype(bf16)
-        twor[q] = rsend(two_out.at[q], two_in.at[q], q, 2, peer)
-        total[q, near] += one_in[q, pl.ds(slot_near * nz, nz)].astype(f32)
-
-    def after_two(q):
-        twor[q].wait_recv()
-        base = block(c, x, y, 0)
-        for j in range(1, nz):
-            zz = lax.rem(z + j, nz)
-            z_out[q, j - 1] = (total[q, base + zz] + two_in[q, zz].astype(f32)).astype(bf16)
+        total[q, near] += core_in[q, pl.ds(block(0, x, y, 0), nz)].astype(f32)
+
+    def after_plane(q):
+        near = pl.ds(block(c, x, y, 0), nz)
+        value = total[q, near]
+        for p in range(3):
+            planer[q, p].wait_recv()
+            value = value + plane_in[q, p * nz : (p + 1) * nz].astype(f32)
+        total[q, near] = value
+        for j in range(1, nz):
+            z_out[q, j - 1] = total[q, block(c, x, y, lax.rem(z + j, nz))].astype(bf16)
             zr[q, j] = rsend(
-                z_out.at[q, j - 1], z_in.at[q, j - 1], q, 2 + j, z_peer(j)
+                z_out.at[q, j - 1], z_in.at[q, j - 1], q, 3 + j, z_peer(j)
             )
-        total[q, base + z] += two_in[q, z].astype(f32)
 
     def finish(q):
         value = total[q, own]
@@ -337,11 +302,57 @@
             value = value + z_in[q, j - 1].astype(f32)
         out_ref[:, pl.ds(q * piece, piece)] = value.astype(out_ref.dtype)
 
-    steps = [produce, after_core, after_one, after_two, finish]
-    for t in range(PIECES + len(steps) - 1):
-        for s, step in enumerate(steps):
-            if 0 <= t - s < PIECES:
-                step(t - s)
+    corners = [(0, 0), (0, 1), (1, 0), (1, 1)]
+
+    def z_first(q):
+        corer[q].wait_recv()
+        for j in range(1, nz):
+            zz = lax.rem(z + j, nz)
+            for g, (xx, yy) in enumerate(corners):
+                plane_out[q, (j - 1) * 4 + g] = (
+                    total[q, block(c, xx, yy, zz)] + core_in[q, block(0, xx, yy, zz)].astype(f32)
+                ).astype(bf16)
+            slots = pl.ds((j - 1) * 4, 4)
+            zr[q, j] = rsend(
+                plane_out.at[q, slots], plane_in.at[q, slots], q, 3 + j, z_peer(j)
+            )
+        for xx, yy in corners:
+            total[q, block(c, xx, yy, z)] += core_in[q, block(0, xx, yy, z)].astype(f32)
+
+    def z_then_plane(q):
+        for j in range(1, nz):
+            zr[q, j].wait_recv()
+        for g, (xx, yy) in enumerate(corners):
+            value = total[q, block(c, xx, yy, z)]
+            for j in range(1, nz):
+                value = value + plane_in[q, (j - 1) * 4 + g].astype(f32)
+            total[q, block(c, xx, yy, z)] = value
+        for p, (xx, yy) in enumerate(plane_at):
+            z_out[q, p] = total[q, block(c, xx, yy, z)].astype(bf16)
+            planer[q, p] = rsend(z_out.at[q, p], z_in.at[q, p], q, 1 + p, plane_peers[p])
+
+    def z_first_finish(q):
+        value = total[q, own]
+        for p in range(3):
+            planer[q, p].wait_recv()
+            value = value + z_in[q, p].astype(f32)
+        out_ref[:, pl.ds(q * piece, piece)] = value.astype(out_ref.dtype)
+
+    for q in range(PIECES):
+        produce(q)
+        if q == 1:
+            z_first(0)
+        elif q:
+            after_core(q - 1)
+    after_core(PIECES - 1)
+    after_plane(1)
+    z_then_plane(0)
+    for q in range(2, PIECES):
+        after_plane(q)
+    finish(1)
+    z_first_finish(0)
+    for q in range(2, PIECES):
+        finish(q)
     for copy in rsends:
         copy.wait_send()
 
@@ -372,15 +383,15 @@
             pltpu.VMEM((per_node, blocks * tok, width), bf16),
             pltpu.VMEM((PIECES, blocks, tok, piece), f32),
             pieces(4 * nz), pieces(4 * nz),
-            pieces(2 * nz), pieces(2 * nz),
-            pieces(nz), pieces(nz),
+            pieces(3 * nz), pieces(3 * nz),
             pieces(nz - 1), pieces(nz - 1),
             dma, dma((per_node,)), dma((per_node,)),
-            dma((2, nz - 1)), dma((2, nz - 1)),
-            dma((2, nz)), dma((2, nz)),
-            dma((2, 2 * nz)), dma((2, 2 * nz)),
-            dma((2, 4)), dma((2, 4)),
-            dma((PIECES, 2 + nz)), dma((PIECES, 2 + nz)),
+            dma((nz - 1,)), dma((nz - 1,)),
+            dma((3,)), dma((3,)),
+            dma((3, nz)), dma((3, nz)),
+            dma((4, nz - 1)), dma((4, nz - 1)),
+            dma((4,)), dma((4,)),
+            dma((PIECES, 3 + nz)), dma((PIECES, 3 + nz)),
         ],
         compiler_params=pltpu.CompilerParams(
             collective_id=0, has_side_effects=True, vmem_limit_bytes=60 * 1024 * 1024
@@ -398,7 +409,7 @@
         if (
             chips == 2
             and nodes == 4 * nz
-            and 2 <= nz <= 4
+            and nz == 4
             and tok == 8
             and model % (PIECES * LANES) == 0
             and experts <= LANES

time: 49.3 us -> 42.4 us (0.86)
  Pallas kernels: 47.6 us -> 40.7 us
    pallas_call x1, Pallas kernels: 47.6 us -> 40.7 us  [fused(): pl.pallas_call(functools.partial(fused_kernel, nz), out_shape=jax.ShapeDt...]
where the time goes in v2:
time: 42.4 us; the launch traced here: 42.2 us
  Pallas kernels  40.7 us (96%)
  local copies, waits for them, and re-layouts  1.45 us (3%)
    pallas_call x1, Pallas kernels, fused(): pl.pallas_call(functools.partial(fused_kernel, nz), out_shape=jax.ShapeDt...  40.7 us
    unnamed x1, local copies, waits for them, and re-layouts  1.45 us

profile of v2, /device:TPU:0, one launch (start us, length us, event | category | flops | bytes accessed | tf_op | source)
XLA Modules:
  0.0 42.2 jit_solution(16217954253176933872)
XLA Ops:
  0.0 40.7 %shard_map.55 = bf16[8,3584]{1,0:T(8,128)(2,1)} custom-call(bf16[8,3584]{1,0:T(8,128)(2,1)} %tokens_ref.1, s32[8,8]{1,0:T(8,128)} %ids_ref.1, bf16[8,8]{1,0:T(8,128)(2,1)} %gates_ref.1, bf16[2,3584,512]{2,1,0:T(8,128)(2,1)} %up_hbm.1, bf16[2,512,3584]{2,1,0:T(8,128)(2,1)} %down_hbm.1), custom_call_target="tpu_custom_call" | custom-call | tf_op jit(solution)/shard_map/pallas_call | solution.py:373
  40.7 1.4 %copy.7 = bf16[8,3584]{1,0:T(8,128)(2,1)} copy(bf16[8,3584]{1,0:T(8,128)(2,1)} %shard_map.55) | data formatting | bytes 114688
